TPU v7x, 512 devices: a whole 4x4x16 slice. The times are simulated.
512 devices in a mesh: row: 32 (over z_hi, x, core), col: 16 (over y, z_lo).
Axes of the slice: x: 4, y: 4, z: 16 (z_hi: 4, z_lo: 4; z = z_hi * 4 + z_lo), core: 2. Of those that a mesh axis runs over, the one named last changes fastest.
Arguments:
- adjoint: bfloat16 [3, 128, 256, 512], P(None, 'col', 'row'), may hold values from -6 to 6
- velocity: bfloat16 [3, 128, 256, 512], P(None, 'col', 'row'), may hold values from -6 to 6
- control: bfloat16 [256, 512], P('row'), may hold values from -6 to 6
- deriv_x: bfloat16 [2, 512, 512], replicated, may hold values from -0.25 to 0.25
- deriv_y: bfloat16 [2, 256, 256], replicated, may hold values from -0.375 to 0.375
- deriv_z: bfloat16 [2, 128, 128], replicated, may hold values from -0.5 to 0.5
Outputs:
- adjoint_rate: bfloat16 [3, 128, 256, 512], P(None, 'col', 'row')
- control_grad: float32 [256, 512], P('row')
All inputs are finite; a program needn't handle non-finite values.
Results may differ from a plain program's by a relative error of at most 0.009.
Values may be sent and summed in bfloat16 or wider, within the bound.
A program may use at most 64 MiB of HBM per device.

v0:
```python
import jax
import jax.numpy as jnp
from jax import lax
from jax.sharding import PartitionSpec as P


def directional(adjoint_in, velocity_in, matrices, component, grid_dim):
    letters = "abcd"
    source = letters[:grid_dim] + "p" + letters[grid_dim + 1 :]
    target = "m" + letters[:grid_dim] + "q" + letters[grid_dim + 1 :]
    stacked = jnp.einsum(
        source + ",mpq->" + target, adjoint_in, matrices, preferred_element_type=jnp.float32
    )
    deriv_term = stacked[0]
    visc_term = stacked[1]
    speeds = velocity_in.astype(jnp.float32)
    summed = visc_term - speeds[component] * deriv_term
    summed = summed.at[component].add(-jnp.sum(speeds * deriv_term, axis=0))
    return summed.astype(jnp.bfloat16)


def on_device(adjoint, velocity, control, deriv_x, deriv_y, deriv_z):
    part_x = directional(adjoint, velocity, deriv_x, 0, 3)
    span_local = jnp.sum(adjoint[0].astype(jnp.float32) * velocity[0].astype(jnp.float32), axis=0)
    control_grad = lax.psum(span_local, "col")
    normal_adj, normal_vel = (
        lax.all_to_all(adjoint, "row", split_axis=3, concat_axis=2, tiled=True),
        lax.all_to_all(velocity, "row", split_axis=3, concat_axis=2, tiled=True),
    )
    part_y = directional(normal_adj, normal_vel, deriv_y, 1, 2)
    span_part = directional(
        lax.all_to_all(normal_adj, "col", split_axis=2, concat_axis=1, tiled=True),
        lax.all_to_all(normal_vel, "col", split_axis=2, concat_axis=1, tiled=True),
        deriv_z,
        2,
        1,
    )
    back_span = lax.all_to_all(span_part, "col", split_axis=1, concat_axis=2, tiled=True)
    side_normal = (part_y.astype(jnp.float32) + back_span.astype(jnp.float32)).astype(jnp.bfloat16)
    side_sum = lax.all_to_all(side_normal, "row", split_axis=2, concat_axis=3, tiled=True)
    summed = part_x.astype(jnp.float32) + side_sum.astype(jnp.float32)
    forcing = control.astype(jnp.float32)[None] * adjoint[0].astype(jnp.float32)
    summed = summed.at[0].add(forcing)
    return (summed.astype(jnp.bfloat16), control_grad)


def solution(mesh):
    in_specs = (
        P(None, "col", "row", None),
        P(None, "col", "row", None),
        P("row", None),
        P(),
        P(),
        P(),
    )
    out_specs = (P(None, "col", "row", None), P("row", None))
    return jax.shard_map(
        on_device, mesh=mesh, in_specs=in_specs, out_specs=out_specs, check_vma=False
    )
```

profile of v0, /device:TPU:4, one launch (start us, length us, event | category | flops | bytes accessed | tf_op | source)
XLA Modules:
  0.0 268.3 jit_solution(13649834393603836144)
XLA Ops:
  0.6 4.4 %copy.52 = bf16[3,8,8,512]{2,1,0,3:T(8,128)(2,1)} copy(bf16[3,8,8,512]{3,2,1,0:T(8,128)(2,1)} %param.15) | data formatting | bytes 393216 | tf_op args[1]
  5.0 5.6 %reshape.186 = bf16[32,2,1536]{2,1,0:T(2,128)(2,1)} reshape(bf16[512,3,8,8]{3,2,1,0:T(8,128)(2,1)} %bitcast.130) | data formatting | bytes 393216
  10.7 18.2 %all-to-all-start.1 = ((bf16[32,2,1536]{2,1,0:T(2,128)(2,1)}), bf16[32,2,1536]{2,1,0:T(2,128)(2,1)S(1)}, u32[]{:S(2)}, u32[]{:S(2)}) async-start(bf16[32,2,1536]{2,1,0:T(2,128)(2,1)} %reshape.186), calls=%async_computation.1 | async-start | bytes 393216 | tf_op jit(solution)/shard_map/all_to_all | solution.py:28
  28.9 3.5 %copy.48 = bf16[3,8,8,512]{2,1,0,3:T(8,128)(2,1)} copy(bf16[3,8,8,512]{3,2,1,0:T(8,128)(2,1)S(1)} %copy-done.2) | data formatting | bytes 393216 | tf_op args[0]
  32.4 5.6 %reshape.182 = bf16[32,2,1536]{2,1,0:T(2,128)(2,1)} reshape(bf16[512,3,8,8]{3,2,1,0:T(8,128)(2,1)} %bitcast.131) | data formatting | bytes 393216
  38.0 8.4 %all-to-all-done.1 = bf16[32,2,1536]{2,1,0:T(2,128)(2,1)S(1)} async-done(((bf16[32,2,1536]{2,1,0:T(2,128)(2,1)}), bf16[32,2,1536]{2,1,0:T(2,128)(2,1)S(1)}, u32[]{:S(2)}, u32[]{:S(2)}) %all-to-all-start.1) | async-done | bytes 196640 | tf_op jit(solution)/shard_map/all_to_all | solution.py:28
  46.4 7.2 %all-to-all-start = ((bf16[32,2,1536]{2,1,0:T(2,128)(2,1)}), bf16[32,2,1536]{2,1,0:T(2,128)(2,1)S(1)}, u32[]{:S(2)}, u32[]{:S(2)}) async-start(bf16[32,2,1536]{2,1,0:T(2,128)(2,1)} %reshape.182), calls=%async_computation | async-start | bytes 393216 | tf_op jit(solution)/shard_map/all_to_all | solution.py:27
  53.6 4.8 %reshape.187 = bf16[512,3,8,8]{3,2,1,0:T(8,128)(2,1)} reshape(bf16[32,2,1536]{2,1,0:T(2,128)(2,1)S(1)} %all-to-all-done.1) | data formatting | bytes 393216
  58.4 4.0 %copy.80 = bf16[3,8,32,8,16]{4,1,0,3,2:T(8,128)(2,1)S(1)} copy(bf16[3,8,32,8,16]{3,1,0,4,2:T(8,128)(2,1)} %bitcast.122) | data formatting | bytes 393216 | tf_op jit(solution)/shard_map/all_to_all | solution.py:28
  62.4 2.3 reshape.188
  64.7 6.3 %all-to-all-done = bf16[32,2,1536]{2,1,0:T(2,128)(2,1)S(1)} async-done(((bf16[32,2,1536]{2,1,0:T(2,128)(2,1)}), bf16[32,2,1536]{2,1,0:T(2,128)(2,1)S(1)}, u32[]{:S(2)}, u32[]{:S(2)}) %all-to-all-start) | async-done | bytes 196640 | tf_op jit(solution)/shard_map/all_to_all | solution.py:27
  71.0 7.4 %all-to-all-start.3 = ((bf16[16,2,3072]{2,1,0:T(2,128)(2,1)}), bf16[16,2,3072]{2,1,0:T(2,128)(2,1)S(1)}, u32[]{:S(2)}, u32[]{:S(2)}) async-start(bf16[16,2,3072]{2,1,0:T(2,128)(2,1)} %reshape.188), calls=%async_computation.3 | async-start | bytes 393216 | tf_op jit(solution)/shard_map/all_to_all | solution.py:33
  78.4 4.8 %reshape.183 = bf16[512,3,8,8]{3,2,1,0:T(8,128)(2,1)} reshape(bf16[32,2,1536]{2,1,0:T(2,128)(2,1)S(1)} %all-to-all-done) | data formatting | bytes 393216
  83.2 4.0 %copy.79 = bf16[3,8,32,8,16]{4,1,0,3,2:T(8,128)(2,1)S(1)} copy(bf16[3,8,32,8,16]{3,1,0,4,2:T(8,128)(2,1)} %bitcast.124) | data formatting | bytes 393216 | tf_op jit(solution)/shard_map/all_to_all | solution.py:27
  87.2 2.3 reshape.184
  89.5 7.5 %all-to-all-start.2 = ((bf16[16,2,3072]{2,1,0:T(2,128)(2,1)}), bf16[16,2,3072]{2,1,0:T(2,128)(2,1)S(1)}, u32[]{:S(2)}, u32[]{:S(2)}) async-start(bf16[16,2,3072]{2,1,0:T(2,128)(2,1)} %reshape.184), calls=%async_computation.2 | async-start | bytes 393216 | tf_op jit(solution)/shard_map/all_to_all | solution.py:32
  97.1 4.8 %copy.50 = bf16[3,8,32,8,16]{4,3,2,1,0:T(8,128)(2,1)} copy(bf16[3,8,32,8,16]{3,1,0,4,2:T(8,128)(2,1)} %bitcast.125) | data formatting | bytes 393216 | tf_op jit(solution)/shard_map/all_to_all | solution.py:27
  101.9 1.2 reshape.189
  103.1 2.1 copy.60
  105.2 2.1 copy.82
  107.3 1.2 reshape.185
  108.4 1.6 copy.57
  110.0 1.9 copy.58
  111.9 2.3 copy.62
  114.2 1.4 slice.167
  116.4 1.0 copy.63
  117.5 2.3 reshape.190
  119.8 7.6 %all-to-all-start.4 = ((bf16[16,2,3072]{2,1,0:T(2,128)(2,1)}), bf16[16,2,3072]{2,1,0:T(2,128)(2,1)}, u32[]{:S(2)}, u32[]{:S(2)}) async-start(bf16[16,2,3072]{2,1,0:T(2,128)(2,1)} %reshape.190), calls=%async_computation.4 | async-start | bytes 393216 | tf_op jit(solution)/shard_map/all_to_all | solution.py:38
  127.4 2.9 %fusion.2 = f32[2,3,8,256,16]{3,4,2,1,0:T(8,128)} fusion(bf16[3,8,32,8,16]{4,3,2,1,0:T(8,128)(2,1)} %copy.50, bf16[2,256,256]{2,1,0:T(8,128)(2,1)S(1)} %copy-done.6), kind=kOutput, calls=%fused_computation.3 | convolution fusion | flops 100663296 | bytes 1245184 | tf_op jit(solution)/shard_map/abpd,mpq->mabqd/dot_general | solution.py:11
  130.3 3.9 %copy.54 = bf16[3,8,32,8,16]{4,3,2,1,0:T(8,128)(2,1)S(1)} copy(bf16[3,8,32,8,16]{3,1,0,4,2:T(8,128)(2,1)} %bitcast.123) | data formatting | bytes 393216 | tf_op jit(solution)/shard_map/all_to_all | solution.py:28
  134.2 0.6 copy.55
  134.8 1.2 multiply_reduce_fusion.1
  136.2 2.3 reshape.191
  138.8 2.0 convert_bitcast_fusion
  140.8 3.7 %copy.65 = f32[3,8,16,16,16]{3,2,4,1,0:T(8,128)} copy(f32[3,8,16,16,16]{4,3,1,2,0:T(8,128)} %convert_bitcast_fusion) | data formatting | bytes 786432 | tf_op jit(solution)/shard_map/convert_element_type | solution.py:39
  144.5 2.8 %reshape.171 = f32[3,8,256,16]{2,3,1,0:T(8,128)S(1)} reshape(f32[3,8,16,16,16]{3,2,4,1,0:T(8,128)} %copy.65) | data formatting | bytes 786432 | tf_op jit(solution)/shard_map/convert_element_type | solution.py:39
  147.4 0.9 copy.66
  148.3 2.4 reshape.192
  150.7 6.8 %all-to-all-start.5 = ((bf16[32,2,1536]{2,1,0:T(2,128)(2,1)}), bf16[32,2,1536]{2,1,0:T(2,128)(2,1)S(1)}, u32[]{:S(2)}, u32[]{:S(2)}) async-start(bf16[32,2,1536]{2,1,0:T(2,128)(2,1)} %reshape.192), calls=%async_computation.5 | async-start | bytes 393216 | tf_op jit(solution)/shard_map/all_to_all | solution.py:40
  158.1 19.1 %all-to-all-done.5 = bf16[32,2,1536]{2,1,0:T(2,128)(2,1)S(1)} async-done(((bf16[32,2,1536]{2,1,0:T(2,128)(2,1)}), bf16[32,2,1536]{2,1,0:T(2,128)(2,1)S(1)}, u32[]{:S(2)}, u32[]{:S(2)}) %all-to-all-start.5) | async-done | bytes 196640 | tf_op jit(solution)/shard_map/all_to_all | solution.py:40
  177.2 1.1 reshape.193
  178.3 0.9 copy.67
  179.2 1.9 copy.68
  181.2 4.1 %copy.69 = f32[3,8,8,32,16]{4,3,2,1,0:T(8,128)} copy(f32[3,8,8,32,16]{4,2,3,1,0:T(8,128)} %bitcast.129) | data formatting | bytes 786432 | tf_op jit(solution)/shard_map/convert_element_type | solution.py:41
  185.3 3.6 %reshape.172 = f32[3,8,8,512]{3,2,1,0:T(8,128)S(1)} reshape(f32[3,8,8,32,16]{4,3,2,1,0:T(8,128)} %copy.69) | data formatting | bytes 786432 | tf_op jit(solution)/shard_map/convert_element_type | solution.py:41
  189.0 0.9 fusion.14
  189.9 77.7 %psum.7 = f32[8,512]{1,0:T(8,128)} all-reduce(f32[8,512]{1,0:T(8,128)S(1)} %get-tuple-element.56), channel_id=1, replica_groups=mesh['row'=32,'col'=16] {'col'}, use_global_device_ids=true, to_apply=%region_4.0 | all-reduce | flops 4096 | bytes 32768 | tf_op jit(solution)/shard_map/psum | solution.py:25
  267.6 0.7 convert_element_type.98
  (34 shorter events, 1.9 us)
Async XLA Ops:
  0.6 156.9 %copy-start = (bf16[2,512,512]{2,1,0:T(8,128)(2,1)S(1)}, bf16[2,512,512]{2,1,0:T(8,128)(2,1)}, u32[]{:S(2)}) copy-start(bf16[2,512,512]{2,1,0:T(8,128)(2,1)} %param.17) | copy-start | bytes 3145732
  5.0 23.9 %copy-start.2 = (bf16[3,8,8,512]{3,2,1,0:T(8,128)(2,1)S(1)}, bf16[3,8,8,512]{3,2,1,0:T(8,128)(2,1)}, u32[]{:S(2)}) copy-start(bf16[3,8,8,512]{3,2,1,0:T(8,128)(2,1)} %param.14) | copy-start | bytes 589828
  10.7 35.7 %all-to-all-start.1 = ((bf16[32,2,1536]{2,1,0:T(2,128)(2,1)}), bf16[32,2,1536]{2,1,0:T(2,128)(2,1)S(1)}, u32[]{:S(2)}, u32[]{:S(2)}) async-start(bf16[32,2,1536]{2,1,0:T(2,128)(2,1)} %reshape.186), calls=%async_computation.1 | async-start | bytes 393216 | tf_op jit(solution)/shard_map/all_to_all | solution.py:28
  46.4 24.6 %all-to-all-start = ((bf16[32,2,1536]{2,1,0:T(2,128)(2,1)}), bf16[32,2,1536]{2,1,0:T(2,128)(2,1)S(1)}, u32[]{:S(2)}, u32[]{:S(2)}) async-start(bf16[32,2,1536]{2,1,0:T(2,128)(2,1)} %reshape.182), calls=%async_computation | async-start | bytes 393216 | tf_op jit(solution)/shard_map/all_to_all | solution.py:27
  71.0 18.5 %all-to-all-start.3 = ((bf16[16,2,3072]{2,1,0:T(2,128)(2,1)}), bf16[16,2,3072]{2,1,0:T(2,128)(2,1)S(1)}, u32[]{:S(2)}, u32[]{:S(2)}) async-start(bf16[16,2,3072]{2,1,0:T(2,128)(2,1)} %reshape.188), calls=%async_computation.3 | async-start | bytes 393216 | tf_op jit(solution)/shard_map/all_to_all | solution.py:33
  87.2 9.9 %copy-start.1 = (bf16[3,8,8,512]{3,2,1,0:T(8,128)(2,1)S(1)}, bf16[3,8,8,512]{3,2,1,0:T(8,128)(2,1)}, u32[]{:S(2)}) copy-start(bf16[3,8,8,512]{3,2,1,0:T(8,128)(2,1)} %param.15) | copy-start | bytes 589828
  87.2 9.9 %copy-start.5 = (bf16[8,512]{1,0:T(8,128)(2,1)S(1)}, bf16[8,512]{1,0:T(8,128)(2,1)}, u32[]{:S(2)}) copy-start(bf16[8,512]{1,0:T(8,128)(2,1)} %param.16) | copy-start | bytes 24580
  89.5 17.8 %all-to-all-start.2 = ((bf16[16,2,3072]{2,1,0:T(2,128)(2,1)}), bf16[16,2,3072]{2,1,0:T(2,128)(2,1)S(1)}, u32[]{:S(2)}, u32[]{:S(2)}) async-start(bf16[16,2,3072]{2,1,0:T(2,128)(2,1)} %reshape.184), calls=%async_computation.2 | async-start | bytes 393216 | tf_op jit(solution)/shard_map/all_to_all | solution.py:32
  114.2 1.8 copy-start.4
  116.4 11.0 %copy-start.6 = (bf16[2,256,256]{2,1,0:T(8,128)(2,1)S(1)}, bf16[2,256,256]{2,1,0:T(8,128)(2,1)}, u32[]{:S(2)}) copy-start(bf16[2,256,256]{2,1,0:T(8,128)(2,1)} %param.18) | copy-start | bytes 786436
  119.8 16.3 %all-to-all-start.4 = ((bf16[16,2,3072]{2,1,0:T(2,128)(2,1)}), bf16[16,2,3072]{2,1,0:T(2,128)(2,1)}, u32[]{:S(2)}, u32[]{:S(2)}) async-start(bf16[16,2,3072]{2,1,0:T(2,128)(2,1)} %reshape.190), calls=%async_computation.4 | async-start | bytes 393216 | tf_op jit(solution)/shard_map/all_to_all | solution.py:38
  147.4 10.1 %copy-start.3 = (bf16[3,8,8,512]{3,2,1,0:T(8,128)(2,1)S(1)}, bf16[3,8,8,512]{3,2,1,0:T(8,128)(2,1)}, u32[]{:S(2)}) copy-start(bf16[3,8,8,512]{3,2,1,0:T(8,128)(2,1)} %param.14) | copy-start | bytes 589828
  150.7 26.5 %all-to-all-start.5 = ((bf16[32,2,1536]{2,1,0:T(2,128)(2,1)}), bf16[32,2,1536]{2,1,0:T(2,128)(2,1)S(1)}, u32[]{:S(2)}, u32[]{:S(2)}) async-start(bf16[32,2,1536]{2,1,0:T(2,128)(2,1)} %reshape.192), calls=%async_computation.5 | async-start | bytes 393216 | tf_op jit(solution)/shard_map/all_to_all | solution.py:40
where the time goes:
time: 270 us; the launch traced here: 268 us
  local copies, waits for them, and re-layouts  92.1 us (34%)
  blocking collectives  77.7 us (29%)
  starting transfers between devices  54.7 us (20%)
  waiting for transfers between devices  33.8 us (13%)
  other arithmetic  5.43 us (2%)
  matrix products  3.54 us (1%)
    psum x1, blocking collectives, on_device(): control_grad = lax.psum(span_local, 'col')  77.7 us
    unnamed x28, local copies, waits for them, and re-layouts  43.8 us
    all_to_all x1, waiting for transfers between devices, on_device(): lax.all_to_all(side_normal, 'row', split_axis=2, concat_axis=3, tiled=True)  19.1 us
    all_to_all x1, starting transfers between devices, on_device(): lax.all_to_all(velocity, 'row', split_axis=3, concat_axis=2, tiled=True)  18.2 us
    convert_element_type x3, local copies, waits for them, and re-layouts, on_device(): summed = part_x.astype(jnp.float32) + side_sum.astype(jnp.float32)  9.7 us
    all_to_all x2, local copies, waits for them, and re-layouts, on_device(): lax.all_to_all(adjoint, 'row', split_axis=3, concat_axis=2, tiled=True)  8.76 us
    all_to_all x3, local copies, waits for them, and re-layouts, on_device(): lax.all_to_all(velocity, 'row', split_axis=3, concat_axis=2, tiled=True)  8.46 us
    all_to_all x1, waiting for transfers between devices, on_device(): lax.all_to_all(velocity, 'row', split_axis=3, concat_axis=2, tiled=True)  8.4 us
  transfers between devices with their start and end apart: 6, of which 3 were waited for; matrix products, arithmetic and copies ran while one was open for 19% of the time, Pallas kernels for 0%

commit v1 on v0

--- a/solution.py
+++ b/solution.py
@@ -20,9 +20,15 @@
 
 
 def on_device(adjoint, velocity, control, deriv_x, deriv_y, deriv_z):
+
+    def _carry_lane(original, lane_axis):
+        state_next = lax.all_gather(original, lane_axis)
+        frame_out = jnp.sum(state_next, axis=0)
+        return frame_out
+
     part_x = directional(adjoint, velocity, deriv_x, 0, 3)
     span_local = jnp.sum(adjoint[0].astype(jnp.float32) * velocity[0].astype(jnp.float32), axis=0)
-    control_grad = lax.psum(span_local, "col")
+    control_grad = _carry_lane(span_local, "col")
     normal_adj, normal_vel = (
         lax.all_to_all(adjoint, "row", split_axis=3, concat_axis=2, tiled=True),
         lax.all_to_all(velocity, "row", split_axis=3, concat_axis=2, tiled=True),

time: 270 us -> 235 us (0.87)
  the two profiles are of different devices: /device:TPU:4 before, /device:TPU:6 now
where the time goes in v1:
time: 235 us; the launch traced here: 234 us
  local copies, waits for them, and re-layouts  92.1 us (39%)
  starting transfers between devices  54.4 us (23%)
  blocking collectives  42.4 us (18%)
  waiting for transfers between devices  34.1 us (15%)
  other arithmetic  6.05 us (3%)
  matrix products  3.54 us (2%)
    unnamed x28, local copies, waits for them, and re-layouts  43.8 us
    all_gather x1, blocking collectives, _carry_lane(): state_next = lax.all_gather(original, lane_axis)  42.4 us
    all_to_all x1, waiting for transfers between devices, on_device(): lax.all_to_all(side_normal, 'row', split_axis=2, concat_axis=3, tiled=True)  19.1 us
    all_to_all x1, starting transfers between devices, on_device(): lax.all_to_all(velocity, 'row', split_axis=3, concat_axis=2, tiled=True)  18.2 us
    convert_element_type x3, local copies, waits for them, and re-layouts, on_device(): summed = part_x.astype(jnp.float32) + side_sum.astype(jnp.float32)  9.7 us
    all_to_all x2, local copies, waits for them, and re-layouts, on_device(): lax.all_to_all(adjoint, 'row', split_axis=3, concat_axis=2, tiled=True)  8.76 us
    all_to_all x3, local copies, waits for them, and re-layouts, on_device(): lax.all_to_all(velocity, 'row', split_axis=3, concat_axis=2, tiled=True)  8.46 us
    all_to_all x1, waiting for transfers between devices, on_device(): lax.all_to_all(velocity, 'row', split_axis=3, concat_axis=2, tiled=True)  8.38 us
  transfers between devices with their start and end apart: 6, of which 4 were waited for; matrix products, arithmetic and copies ran while one was open for 22% of the time, Pallas kernels for 0%

profile of v1, /device:TPU:6, one launch (start us, length us, event | category | flops | bytes accessed | tf_op | source)
XLA Modules:
  0.0 233.6 jit_solution(735528473565167458)
XLA Ops:
  0.6 4.4 %copy.73 = bf16[3,8,8,512]{2,1,0,3:T(8,128)(2,1)} copy(bf16[3,8,8,512]{3,2,1,0:T(8,128)(2,1)} %param.15) | data formatting | bytes 393216 | tf_op args[1]
  5.0 5.6 %reshape.187 = bf16[32,2,1536]{2,1,0:T(2,128)(2,1)} reshape(bf16[512,3,8,8]{3,2,1,0:T(8,128)(2,1)} %bitcast.132) | data formatting | bytes 393216
  10.7 18.2 %all-to-all-start.1 = ((bf16[32,2,1536]{2,1,0:T(2,128)(2,1)}), bf16[32,2,1536]{2,1,0:T(2,128)(2,1)S(1)}, u32[]{:S(2)}, u32[]{:S(2)}) async-start(bf16[32,2,1536]{2,1,0:T(2,128)(2,1)} %reshape.187), calls=%async_computation.1 | async-start | bytes 393216 | tf_op jit(solution)/shard_map/all_to_all | solution.py:34
  28.9 3.5 %copy.69 = bf16[3,8,8,512]{2,1,0,3:T(8,128)(2,1)} copy(bf16[3,8,8,512]{3,2,1,0:T(8,128)(2,1)S(1)} %copy-done.2) | data formatting | bytes 393216 | tf_op args[0]
  32.4 5.6 %reshape.183 = bf16[32,2,1536]{2,1,0:T(2,128)(2,1)} reshape(bf16[512,3,8,8]{3,2,1,0:T(8,128)(2,1)} %bitcast.133) | data formatting | bytes 393216
  38.0 8.4 %all-to-all-done.1 = bf16[32,2,1536]{2,1,0:T(2,128)(2,1)S(1)} async-done(((bf16[32,2,1536]{2,1,0:T(2,128)(2,1)}), bf16[32,2,1536]{2,1,0:T(2,128)(2,1)S(1)}, u32[]{:S(2)}, u32[]{:S(2)}) %all-to-all-start.1) | async-done | bytes 196640 | tf_op jit(solution)/shard_map/all_to_all | solution.py:34
  46.4 7.2 %all-to-all-start = ((bf16[32,2,1536]{2,1,0:T(2,128)(2,1)}), bf16[32,2,1536]{2,1,0:T(2,128)(2,1)S(1)}, u32[]{:S(2)}, u32[]{:S(2)}) async-start(bf16[32,2,1536]{2,1,0:T(2,128)(2,1)} %reshape.183), calls=%async_computation | async-start | bytes 393216 | tf_op jit(solution)/shard_map/all_to_all | solution.py:33
  53.6 4.8 %reshape.188 = bf16[512,3,8,8]{3,2,1,0:T(8,128)(2,1)} reshape(bf16[32,2,1536]{2,1,0:T(2,128)(2,1)S(1)} %all-to-all-done.1) | data formatting | bytes 393216
  58.3 4.0 %copy.101 = bf16[3,8,32,8,16]{4,1,0,3,2:T(8,128)(2,1)S(1)} copy(bf16[3,8,32,8,16]{3,1,0,4,2:T(8,128)(2,1)} %bitcast.124) | data formatting | bytes 393216 | tf_op jit(solution)/shard_map/all_to_all | solution.py:34
  62.3 2.3 %reshape.189 = bf16[16,2,3072]{2,1,0:T(2,128)(2,1)} reshape(bf16[256,3,8,16]{3,2,1,0:T(8,128)(2,1)S(1)} %bitcast.142) | data formatting | bytes 393216
  64.7 6.3 %all-to-all-done = bf16[32,2,1536]{2,1,0:T(2,128)(2,1)S(1)} async-done(((bf16[32,2,1536]{2,1,0:T(2,128)(2,1)}), bf16[32,2,1536]{2,1,0:T(2,128)(2,1)S(1)}, u32[]{:S(2)}, u32[]{:S(2)}) %all-to-all-start) | async-done | bytes 196640 | tf_op jit(solution)/shard_map/all_to_all | solution.py:33
  71.0 7.3 %all-to-all-start.3 = ((bf16[16,2,3072]{2,1,0:T(2,128)(2,1)}), bf16[16,2,3072]{2,1,0:T(2,128)(2,1)S(1)}, u32[]{:S(2)}, u32[]{:S(2)}) async-start(bf16[16,2,3072]{2,1,0:T(2,128)(2,1)} %reshape.189), calls=%async_computation.3 | async-start | bytes 393216 | tf_op jit(solution)/shard_map/all_to_all | solution.py:39
  78.3 4.8 %reshape.184 = bf16[512,3,8,8]{3,2,1,0:T(8,128)(2,1)} reshape(bf16[32,2,1536]{2,1,0:T(2,128)(2,1)S(1)} %all-to-all-done) | data formatting | bytes 393216
  83.1 4.0 %copy.100 = bf16[3,8,32,8,16]{4,1,0,3,2:T(8,128)(2,1)S(1)} copy(bf16[3,8,32,8,16]{3,1,0,4,2:T(8,128)(2,1)} %bitcast.126) | data formatting | bytes 393216 | tf_op jit(solution)/shard_map/all_to_all | solution.py:33
  87.1 2.3 %reshape.185 = bf16[16,2,3072]{2,1,0:T(2,128)(2,1)} reshape(bf16[256,3,8,16]{3,2,1,0:T(8,128)(2,1)S(1)} %bitcast.143) | data formatting | bytes 393216
  89.5 7.5 %all-to-all-start.2 = ((bf16[16,2,3072]{2,1,0:T(2,128)(2,1)}), bf16[16,2,3072]{2,1,0:T(2,128)(2,1)S(1)}, u32[]{:S(2)}, u32[]{:S(2)}) async-start(bf16[16,2,3072]{2,1,0:T(2,128)(2,1)} %reshape.185), calls=%async_computation.2 | async-start | bytes 393216 | tf_op jit(solution)/shard_map/all_to_all | solution.py:38
  97.1 4.8 %copy.71 = bf16[3,8,32,8,16]{4,3,2,1,0:T(8,128)(2,1)} copy(bf16[3,8,32,8,16]{3,1,0,4,2:T(8,128)(2,1)} %bitcast.127) | data formatting | bytes 393216 | tf_op jit(solution)/shard_map/all_to_all | solution.py:33
  101.8 1.2 reshape.190
  103.0 2.1 copy.81
  105.1 2.1 copy.103
  107.2 1.2 reshape.186
  108.4 1.6 copy.78
  109.9 1.9 copy.79
  111.8 2.3 copy.83
  114.1 1.4 slice.167
  116.4 1.0 copy.84
  117.4 2.3 %reshape.191 = bf16[16,2,3072]{2,1,0:T(2,128)(2,1)} reshape(bf16[128,3,16,16]{3,2,1,0:T(8,128)(2,1)S(1)} %bitcast.136) | data formatting | bytes 393216
  119.7 7.6 %all-to-all-start.4 = ((bf16[16,2,3072]{2,1,0:T(2,128)(2,1)}), bf16[16,2,3072]{2,1,0:T(2,128)(2,1)}, u32[]{:S(2)}, u32[]{:S(2)}) async-start(bf16[16,2,3072]{2,1,0:T(2,128)(2,1)} %reshape.191), calls=%async_computation.4 | async-start | bytes 393216 | tf_op jit(solution)/shard_map/all_to_all | solution.py:44
  127.3 2.9 %fusion.2 = f32[2,3,8,256,16]{3,4,2,1,0:T(8,128)} fusion(bf16[3,8,32,8,16]{4,3,2,1,0:T(8,128)(2,1)} %copy.71, bf16[2,256,256]{2,1,0:T(8,128)(2,1)S(1)} %copy-done.6), kind=kOutput, calls=%fused_computation.3 | convolution fusion | flops 100663296 | bytes 1245184 | tf_op jit(solution)/shard_map/abpd,mpq->mabqd/dot_general | solution.py:11
  130.2 3.9 %copy.75 = bf16[3,8,32,8,16]{4,3,2,1,0:T(8,128)(2,1)S(1)} copy(bf16[3,8,32,8,16]{3,1,0,4,2:T(8,128)(2,1)} %bitcast.125) | data formatting | bytes 393216 | tf_op jit(solution)/shard_map/all_to_all | solution.py:34
  134.8 1.2 multiply_reduce_fusion.1
  136.3 2.3 reshape.192
  138.9 2.0 convert_bitcast_fusion
  140.9 3.7 %copy.86 = f32[3,8,16,16,16]{3,2,4,1,0:T(8,128)} copy(f32[3,8,16,16,16]{4,3,1,2,0:T(8,128)} %convert_bitcast_fusion) | data formatting | bytes 786432 | tf_op jit(solution)/shard_map/convert_element_type | solution.py:45
  144.7 2.8 %reshape.171 = f32[3,8,256,16]{2,3,1,0:T(8,128)S(1)} reshape(f32[3,8,16,16,16]{3,2,4,1,0:T(8,128)} %copy.86) | data formatting | bytes 786432 | tf_op jit(solution)/shard_map/convert_element_type | solution.py:45
  147.5 0.9 copy.87
  148.5 2.4 %reshape.193 = bf16[32,2,1536]{2,1,0:T(2,128)(2,1)} reshape(bf16[256,3,8,16]{3,2,1,0:T(8,128)(2,1)S(1)} %bitcast.138) | data formatting | bytes 393216
  150.8 6.7 %all-to-all-start.5 = ((bf16[32,2,1536]{2,1,0:T(2,128)(2,1)}), bf16[32,2,1536]{2,1,0:T(2,128)(2,1)S(1)}, u32[]{:S(2)}, u32[]{:S(2)}) async-start(bf16[32,2,1536]{2,1,0:T(2,128)(2,1)} %reshape.193), calls=%async_computation.5 | async-start | bytes 393216 | tf_op jit(solution)/shard_map/all_to_all | solution.py:46
  158.0 19.1 %all-to-all-done.5 = bf16[32,2,1536]{2,1,0:T(2,128)(2,1)S(1)} async-done(((bf16[32,2,1536]{2,1,0:T(2,128)(2,1)}), bf16[32,2,1536]{2,1,0:T(2,128)(2,1)S(1)}, u32[]{:S(2)}, u32[]{:S(2)}) %all-to-all-start.5) | async-done | bytes 196640 | tf_op jit(solution)/shard_map/all_to_all | solution.py:46
  177.2 1.1 reshape.194
  178.3 0.9 copy.88
  179.2 1.9 copy.89
  181.1 4.1 %copy.90 = f32[3,8,8,32,16]{4,3,2,1,0:T(8,128)} copy(f32[3,8,8,32,16]{4,2,3,1,0:T(8,128)} %bitcast.131) | data formatting | bytes 786432 | tf_op jit(solution)/shard_map/convert_element_type | solution.py:47
  185.3 3.6 %reshape.172 = f32[3,8,8,512]{3,2,1,0:T(8,128)S(1)} reshape(f32[3,8,8,32,16]{4,3,2,1,0:T(8,128)} %copy.90) | data formatting | bytes 786432 | tf_op jit(solution)/shard_map/convert_element_type | solution.py:47
  189.0 0.9 fusion.14
  189.9 0.7 convert_element_type.98
  190.6 42.4 %all-gather = f32[128,512]{1,0:T(8,128)S(1)} all-gather(f32[8,512]{1,0:T(8,128)S(1)} %get-tuple-element.56), channel_id=2, replica_groups=mesh['row'=32,'col'=16] {'col'}, dimensions={0}, use_global_device_ids=true | all-gather | bytes 278528 | tf_op jit(solution)/shard_map/all_gather | solution.py:25
  233.0 0.6 bitcast_reduce_fusion
  (35 shorter events, 2.7 us)
Async XLA Ops:
  0.6 156.9 %copy-start = (bf16[2,512,512]{2,1,0:T(8,128)(2,1)S(1)}, bf16[2,512,512]{2,1,0:T(8,128)(2,1)}, u32[]{:S(2)}) copy-start(bf16[2,512,512]{2,1,0:T(8,128)(2,1)} %param.17) | copy-start | bytes 3145732
  5.0 23.8 %copy-start.2 = (bf16[3,8,8,512]{3,2,1,0:T(8,128)(2,1)S(1)}, bf16[3,8,8,512]{3,2,1,0:T(8,128)(2,1)}, u32[]{:S(2)}) copy-start(bf16[3,8,8,512]{3,2,1,0:T(8,128)(2,1)} %param.14) | copy-start | bytes 589828
  10.7 35.7 %all-to-all-start.1 = ((bf16[32,2,1536]{2,1,0:T(2,128)(2,1)}), bf16[32,2,1536]{2,1,0:T(2,128)(2,1)S(1)}, u32[]{:S(2)}, u32[]{:S(2)}) async-start(bf16[32,2,1536]{2,1,0:T(2,128)(2,1)} %reshape.187), calls=%async_computation.1 | async-start | bytes 393216 | tf_op jit(solution)/shard_map/all_to_all | solution.py:34
  46.4 24.6 %all-to-all-start = ((bf16[32,2,1536]{2,1,0:T(2,128)(2,1)}), bf16[32,2,1536]{2,1,0:T(2,128)(2,1)S(1)}, u32[]{:S(2)}, u32[]{:S(2)}) async-start(bf16[32,2,1536]{2,1,0:T(2,128)(2,1)} %reshape.183), calls=%async_computation | async-start | bytes 393216 | tf_op jit(solution)/shard_map/all_to_all | solution.py:33
  71.0 18.5 %all-to-all-start.3 = ((bf16[16,2,3072]{2,1,0:T(2,128)(2,1)}), bf16[16,2,3072]{2,1,0:T(2,128)(2,1)S(1)}, u32[]{:S(2)}, u32[]{:S(2)}) async-start(bf16[16,2,3072]{2,1,0:T(2,128)(2,1)} %reshape.189), calls=%async_computation.3 | async-start | bytes 393216 | tf_op jit(solution)/shard_map/all_to_all | solution.py:39
  87.1 9.9 %copy-start.1 = (bf16[3,8,8,512]{3,2,1,0:T(8,128)(2,1)S(1)}, bf16[3,8,8,512]{3,2,1,0:T(8,128)(2,1)}, u32[]{:S(2)}) copy-start(bf16[3,8,8,512]{3,2,1,0:T(8,128)(2,1)} %param.15) | copy-start | bytes 589828
  87.1 9.9 %copy-start.5 = (bf16[8,512]{1,0:T(8,128)(2,1)S(1)}, bf16[8,512]{1,0:T(8,128)(2,1)}, u32[]{:S(2)}) copy-start(bf16[8,512]{1,0:T(8,128)(2,1)} %param.16) | copy-start | bytes 24580
  89.5 17.8 %all-to-all-start.2 = ((bf16[16,2,3072]{2,1,0:T(2,128)(2,1)}), bf16[16,2,3072]{2,1,0:T(2,128)(2,1)S(1)}, u32[]{:S(2)}, u32[]{:S(2)}) async-start(bf16[16,2,3072]{2,1,0:T(2,128)(2,1)} %reshape.185), calls=%async_computation.2 | async-start | bytes 393216 | tf_op jit(solution)/shard_map/all_to_all | solution.py:38
  114.1 1.8 copy-start.4
  116.3 11.0 %copy-start.6 = (bf16[2,256,256]{2,1,0:T(8,128)(2,1)S(1)}, bf16[2,256,256]{2,1,0:T(8,128)(2,1)}, u32[]{:S(2)}) copy-start(bf16[2,256,256]{2,1,0:T(8,128)(2,1)} %param.18) | copy-start | bytes 786436
  119.7 16.6 %all-to-all-start.4 = ((bf16[16,2,3072]{2,1,0:T(2,128)(2,1)}), bf16[16,2,3072]{2,1,0:T(2,128)(2,1)}, u32[]{:S(2)}, u32[]{:S(2)}) async-start(bf16[16,2,3072]{2,1,0:T(2,128)(2,1)} %reshape.191), calls=%async_computation.4 | async-start | bytes 393216 | tf_op jit(solution)/shard_map/all_to_all | solution.py:44
  147.5 10.0 %copy-start.3 = (bf16[3,8,8,512]{3,2,1,0:T(8,128)(2,1)S(1)}, bf16[3,8,8,512]{3,2,1,0:T(8,128)(2,1)}, u32[]{:S(2)}) copy-start(bf16[3,8,8,512]{3,2,1,0:T(8,128)(2,1)} %param.14) | copy-start | bytes 589828
  150.8 26.4 %all-to-all-start.5 = ((bf16[32,2,1536]{2,1,0:T(2,128)(2,1)}), bf16[32,2,1536]{2,1,0:T(2,128)(2,1)S(1)}, u32[]{:S(2)}, u32[]{:S(2)}) async-start(bf16[32,2,1536]{2,1,0:T(2,128)(2,1)} %reshape.193), calls=%async_computation.5 | async-start | bytes 393216 | tf_op jit(solution)/shard_map/all_to_all | solution.py:46
